TPU v7x, 256 devices: a whole 4x4x8 slice. The times are simulated.
256 devices in a mesh: strip: 8 (over x, core), sub: 32 (over z, y).
Axes of the slice: x: 4, y: 4, z: 8, core: 2. Of those that a mesh axis runs over, the one named last changes fastest.
Arguments:
- node_latents: bfloat16 [65536, 128], P(('strip', 'sub')), may hold values from -6 to 6
- edge_latents: bfloat16 [1048576, 128], P(('strip', 'sub')), may hold values from -6 to 6
- senders: int32 [1048576], P(('strip', 'sub')), may hold values from 0 to 65535, as said below
- receivers: int32 [1048576], P(('strip', 'sub')), may hold values from 0 to 255
- edge_count: int32 [256], P(('strip', 'sub')), may hold values from 1024 to 4096, as said below
- w_edge_in: bfloat16 [384, 128], replicated, may hold values from -0.3125 to 0.3125
- w_edge_out: bfloat16 [128, 128], replicated, may hold values from -0.5 to 0.5
- w_node_in: bfloat16 [256, 128], replicated, may hold values from -0.375 to 0.375
- w_node_out: bfloat16 [128, 128], replicated, may hold values from -0.5 to 0.5
- node_cotangent: bfloat16 [65536, 128], P(('strip', 'sub')), may hold values from -6 to 6
- edge_cotangent: bfloat16 [1048576, 128], P(('strip', 'sub')), may hold values from -6 to 6
Outputs:
- new_nodes: bfloat16 [65536, 128], P(('strip', 'sub'))
- new_edges: bfloat16 [1048576, 128], P(('strip', 'sub'))
- node_grad: float32 [65536, 128], P(('strip', 'sub'))
- grad_edge_in: float32 [384, 128], replicated
- grad_edge_out: float32 [128, 128], replicated
- grad_node_in: float32 [256, 128], replicated
- grad_node_out: float32 [128, 128], replicated
Inputs may be any that keep to these rules, and one draw needn't show every extreme that they name: `senders`: devices are numbered strip * 32 + sub-block, each holding 256 consecutive particles and 4096 consecutive edge slots. The sender of an edge held by the device at strip i and sub-block j is a particle of a device at strip i - 1, i or i + 1 and sub-block j - 1, j or j + 1 (no wrap); if that device is not the edge's own, the sender is among its first 32 particles. A device's live edges are its first edge_count slots; some device is full.
All inputs are finite; a program needn't handle non-finite values.
Results may differ from a plain program's by a relative error of at most 0.012.
Values may be sent and summed in bfloat16 or wider, within the bound.
A program may use at most 64 MiB of HBM per device.

v0:
```python
import math

import jax
import jax.numpy as jnp
from jax import lax
from jax.sharding import PartitionSpec as P

EPS = 1e-05


def padded_2(block, sides, width):
    for axis, dim in sides:
        count = lax.axis_size(axis)
        forward = [(i, i + 1) for i in range(count - 1)]
        backward = [(target, source) for source, target in forward]
        low = lax.ppermute(
            lax.slice_in_dim(block, block.shape[dim] - width, None, axis=dim), axis, forward
        )
        high = lax.ppermute(lax.slice_in_dim(block, 0, width, axis=dim), axis, backward)
        block = jnp.concatenate([low, block, high], axis=dim)
    return block


def shifted(value, axis, steps):
    count = lax.axis_size(axis)
    first, last = (max(0, -steps), min(count, count - steps))
    return lax.ppermute(value, axis, [(source, source + steps) for source in range(first, last)])


def norm_rows(values):
    centre = values - jnp.mean(values, axis=1, keepdims=True)
    scale = lax.rsqrt(jnp.mean(centre * centre, axis=1, keepdims=True) + EPS)
    return (centre * scale, scale)


def norm_back(normed, scale, upstream):
    first = jnp.mean(upstream, axis=1, keepdims=True)
    second = jnp.mean(upstream * normed, axis=1, keepdims=True)
    return scale * (upstream - first - normed * second)


def silu_grad(values):
    sig = jax.nn.sigmoid(values)
    return sig * (1.0 + values * (1.0 - sig))


def pick_rows(onehot, table):
    return jnp.dot(onehot, table, preferred_element_type=jnp.float32)


def pick_exact(onehot, table):
    return jnp.dot(
        onehot.astype(jnp.float32),
        table,
        precision=lax.Precision.HIGHEST,
        preferred_element_type=jnp.float32,
    )


def sum_rows(onehot, values):
    return jnp.dot(
        onehot.astype(jnp.float32).T,
        values,
        precision=lax.Precision.HIGHEST,
        preferred_element_type=jnp.float32,
    )


def shards(
    node_latents,
    edge_latents,
    senders,
    receivers,
    edge_count,
    w_edge_in,
    w_edge_out,
    w_node_in,
    w_node_out,
    node_cotangent,
    edge_cotangent,
):
    count_p = node_latents.shape[0]
    width = node_latents.shape[1]
    count_e = edge_latents.shape[0]
    border = count_p // 8
    subs_here = lax.axis_size("sub")
    my_strip = lax.axis_index("strip")
    my_sub = lax.axis_index("sub")
    rim_rows = node_latents[:border].reshape(1, 1, border, width)
    padded = padded_2(rim_rows, (("strip", 0), ("sub", 1)), 1)
    table = jnp.concatenate([node_latents, padded.reshape(9 * border, width)], axis=0)
    owner = senders // count_p
    within = senders % count_p
    is_local = owner == my_strip * subs_here + my_sub
    block = (owner // subs_here - my_strip + 1) * 3 + (owner % subs_here - my_sub + 1)
    send_index = jnp.where(
        is_local, within, count_p + block * border + jnp.minimum(within, border - 1)
    )
    valid = (jnp.arange(count_e, dtype=jnp.int32) < edge_count[0]).astype(jnp.float32)
    send_hot = (
        send_index[:, None] == jnp.arange(count_p + 9 * border, dtype=jnp.int32)[None, :]
    ).astype(jnp.bfloat16)
    recv_hot = (receivers[:, None] == jnp.arange(count_p, dtype=jnp.int32)[None, :]).astype(
        jnp.bfloat16
    )
    send_rows = pick_rows(send_hot, table).astype(jnp.bfloat16)
    recv_rows = pick_rows(recv_hot, node_latents).astype(jnp.bfloat16)
    stacked = jnp.concatenate([send_rows, recv_rows, edge_latents], axis=1)
    hidden_pre = jnp.dot(stacked, w_edge_in, preferred_element_type=jnp.float32)
    hidden = jax.nn.silu(hidden_pre).astype(jnp.bfloat16)
    outer = jnp.dot(hidden, w_edge_out, preferred_element_type=jnp.float32)
    normed, scale = norm_rows(outer)
    message = normed * valid[:, None]
    new_edges = (edge_latents.astype(jnp.float32) + message).astype(jnp.bfloat16)
    agg = sum_rows(recv_hot, message)
    joined = jnp.concatenate([node_latents, agg.astype(jnp.bfloat16)], axis=1)
    node_pre = jnp.dot(joined, w_node_in, preferred_element_type=jnp.float32)
    node_act = jax.nn.silu(node_pre).astype(jnp.bfloat16)
    node_outer = jnp.dot(node_act, w_node_out, preferred_element_type=jnp.float32)
    node_normed, node_scale = norm_rows(node_outer)
    new_nodes = (node_latents.astype(jnp.float32) + node_normed).astype(jnp.bfloat16)
    node_cot = node_cotangent.astype(jnp.float32)
    d_node_outer = norm_back(node_normed, node_scale, node_cot).astype(jnp.bfloat16)
    gn_out = jnp.dot(node_act.T, d_node_outer, preferred_element_type=jnp.float32)
    d_node_act = jnp.dot(d_node_outer, w_node_out.T, preferred_element_type=jnp.float32)
    d_node_pre = (d_node_act * silu_grad(node_pre)).astype(jnp.bfloat16)
    gn_in = jnp.dot(joined.T, d_node_pre, preferred_element_type=jnp.float32)
    d_joined = jnp.dot(d_node_pre, w_node_in.T, preferred_element_type=jnp.float32)
    upstream = edge_cotangent.astype(jnp.float32) + pick_exact(recv_hot, d_joined[:, width:])
    d_outer = norm_back(normed, scale, upstream * valid[:, None]).astype(jnp.bfloat16)
    ge_out = jnp.dot(hidden.T, d_outer, preferred_element_type=jnp.float32)
    d_hidden = jnp.dot(d_outer, w_edge_out.T, preferred_element_type=jnp.float32)
    d_pre = (d_hidden * silu_grad(hidden_pre)).astype(jnp.bfloat16)
    ge_in = jnp.dot(stacked.T, d_pre, preferred_element_type=jnp.float32)
    d_stacked = jnp.dot(d_pre, w_edge_in.T, preferred_element_type=jnp.float32)
    send_sums = sum_rows(send_hot, d_stacked[:, :width])
    owed = send_sums[count_p:].reshape(3, 3, border, width)
    local_grad = (
        node_cot
        + d_joined[:, :width]
        + sum_rows(recv_hot, d_stacked[:, width : 2 * width])
        + send_sums[:count_p]
    )
    column = (
        owed[:, 1]
        + shifted(owed[:, 0].astype(jnp.bfloat16), "sub", -1).astype(jnp.float32)
        + shifted(owed[:, 2].astype(jnp.bfloat16), "sub", 1).astype(jnp.float32)
    )
    returned = column[1] + shifted(column[0], "strip", -1) + shifted(column[2], "strip", 1)
    node_grad = local_grad.at[:border].add(returned)
    totals = lax.psum((ge_in, ge_out, gn_in, gn_out), ("strip", "sub"))
    factor = 1.0 / math.sqrt(count_e * lax.axis_size("strip") * subs_here)
    return (
        new_nodes,
        new_edges,
        node_grad,
        totals[0] * factor,
        totals[1] * factor,
        totals[2] * factor,
        totals[3] * factor,
    )


def solution(mesh):
    placed = (
        P(("strip", "sub"), None),
        P(("strip", "sub"), None),
        P(("strip", "sub")),
        P(("strip", "sub")),
        P(("strip", "sub")),
        P(),
        P(),
        P(),
        P(),
        P(("strip", "sub"), None),
        P(("strip", "sub"), None),
    )
    return jax.shard_map(
        shards,
        mesh=mesh,
        in_specs=placed,
        out_specs=(
            P(("strip", "sub"), None),
            P(("strip", "sub"), None),
            P(("strip", "sub"), None),
            P(),
            P(),
            P(),
            P(),
        ),
        check_vma=False,
    )
```

profile of v0, /device:TPU:1, one launch (start us, length us, event | category | flops | bytes accessed | tf_op | source)
XLA Modules:
  0.0 340.3 jit_solution(2985765691667159011)
XLA Ops:
  8.1 5.1 %collective-permute-start.1 = (bf16[1,1,32,128]{3,2,1,0:T(8,128)(2,1)S(1)}, bf16[1,1,32,128]{3,2,1,0:T(8,128)(2,1)S(1)}, u32[]{:S(2)}, u32[]{:S(2)}) collective-permute-start(bf16[1,1,32,128]{3,2,1,0:T(8,128)(2,1)S(1)} %slice_bitcast_fusion.6), channel_id=1, source_target_pairs={{32,0},{64,32},{96,64},{128,96},{160,128},{192,160},{224,192},{33,... | collective-permute-start | bytes 24584 | tf_op jit(solution)/shard_map/ppermute | solution.py:19
  13.2 1.9 collective-permute-start
  15.1 2.9 convolution_convert_fusion
  19.4 1.3 collective-permute-start.3
  20.7 4.0 %collective-permute-start.2 = (bf16[3,1,32,128]{3,2,1,0:T(8,128)(2,1)S(1)}, bf16[3,1,32,128]{3,2,1,0:T(8,128)(2,1)S(1)}, u32[]{:S(2)}, u32[]{:S(2)}) collective-permute-start(bf16[3,1,32,128]{3,2,1,0:T(8,128)(2,1)S(1)} %pad_maximum_fusion.7), channel_id=1, source_target_pairs={{0,1},{1,2},{2,3},{3,4},{4,5},{5,6},{6,7},{7,8},{8,9},{9,10},{10,1... | collective-permute-start | bytes 73736 | tf_op jit(solution)/shard_map/ppermute | solution.py:16
  26.1 2.9 fusion.4
  29.0 1.6 multiply_convert_fusion.1
  31.4 1.9 fusion.24
  34.5 2.6 fusion.67
  37.8 1.1 fusion.72
  39.9 1.7 fusion.16
  41.6 1.0 fusion.71
  42.6 4.5 %fusion = f32[544,128]{1,0:T(8,128)S(1)} fusion(s32[4096]{0:T(1024)S(1)} %copy-done.11, f32[4096,384]{1,0:T(8,128)S(1)} %fusion.71), kind=kOutput, calls=%fused_computation.1 | convolution fusion | flops 3424780288 | bytes 2392064 | tf_op jit(solution)/shard_map/dot_general | solution.py:61
  47.7 1.3 collective-permute-start.4
  49.0 4.0 %collective-permute-start.5 = (bf16[3,32,128]{1,2,0:T(8,128)(2,1)S(1)}, bf16[3,32,128]{1,2,0:T(8,128)(2,1)S(1)}, u32[]{:S(2)}, u32[]{:S(2)}) collective-permute-start(bf16[3,32,128]{1,2,0:T(8,128)(2,1)S(1)} %get-tuple-element.51), channel_id=1, source_target_pairs={{0,1},{1,2},{2,3},{3,4},{4,5},{5,6},{6,7},{7,8},{8,9},{9,10},{10,1... | collective-permute-start | bytes 73736 | tf_op jit(solution)/shard_map/ppermute | solution.py:27
  53.0 4.0 %fusion.21 = f32[256,128]{0,1:T(8,128)S(1)} fusion(f32[256,128]{0,1:T(8,128)S(1)} %copy.60, f32[4096,384]{1,0:T(8,128)} %copy-done.1, s32[4096]{0:T(1024)S(1)} %copy-done.12, f32[256,128]{0,1:T(8,128)S(1)} %copy.59, bf16[256,128]{0,1:T(8,128)(2,1)S(1)} %copy.48), kind=kOutput, calls=%fused_computation.32 | convolution fusion | flops 1611792384 | bytes 2572288 | tf_op jit(solution)/shard_map/dot_general | solution.py:61
  57.8 3.9 %collective-permute-start.6 = (f32[32,128]{0,1:T(8,128)S(1)}, f32[32,128]{0,1:T(8,128)S(1)}, u32[]{:S(2)}, u32[]{:S(2)}) collective-permute-start(f32[32,128]{0,1:T(8,128)S(1)} %get-tuple-element.52), channel_id=1, source_target_pairs={{32,0},{64,32},{96,64},{128,96},{160,128},{192,160},{224,192},{33,... | collective-permute-start | bytes 49160 | tf_op jit(solution)/shard_map/ppermute | solution.py:27
  61.8 1.9 collective-permute-start.7
  65.3 1.3 copy.56
  68.1 259.2 %all-reduce.3.cloned.1.call-done = (f32[384,128]{1,0:T(8,128)}, f32[128,128]{1,0:T(8,128)}, f32[256,128]{1,0:T(8,128)}, f32[128,128]{1,0:T(8,128)}) async-done(((f32[384,128]{1,0:T(8,128)}, f32[128,128]{1,0:T(8,128)}, f32[256,128]{1,0:T(8,128)}, f32[128,128]{1,0:T(8,128)}), (f32[384,128]{1,0:T(8,128)}, f32[128,128]{1,0:T(8,128)}, f32[256,128]{1,0:T(8,128)}, ...) | async-done | bytes 458768 | tf_op jit(solution)/shard_map/psum | solution.py:151
  327.3 1.6 broadcast_multiply_fusion
  328.9 1.5 broadcast_multiply_fusion.3
  330.4 1.5 broadcast_multiply_fusion.2
  331.9 1.6 broadcast_multiply_fusion.1
  (82 shorter events, 10.7 us)
Async XLA Ops:
  7.2 21.8 %copy-start = (bf16[384,128]{1,0:T(8,128)(2,1)S(1)}, bf16[384,128]{1,0:T(8,128)(2,1)}, u32[]{:S(2)}) copy-start(bf16[384,128]{1,0:T(8,128)(2,1)} %param.18) | copy-start | bytes 294916
  7.2 17.5 %copy-start.5 = (bf16[256,128]{1,0:T(8,128)(2,1)S(1)}, bf16[256,128]{1,0:T(8,128)(2,1)}, u32[]{:S(2)}) copy-start(bf16[256,128]{1,0:T(8,128)(2,1)} %param.13) | copy-start | bytes 196612
  7.2 10.8 %copy-start.10 = (s32[4096]{0:T(1024)S(1)}, s32[4096]{0:T(1024)}, u32[]{:S(2)}) copy-start(s32[4096]{0:T(1024)} %param.15) | copy-start | bytes 49156
  7.2 17.6 %copy-start.6 = (bf16[256,128]{1,0:T(8,128)(2,1)S(1)}, bf16[256,128]{1,0:T(8,128)(2,1)}, u32[]{:S(2)}) copy-start(bf16[256,128]{1,0:T(8,128)(2,1)} %param.22) | copy-start | bytes 196612
  7.2 17.7 %copy-start.2 = (bf16[4096,128]{1,0:T(8,128)(2,1)S(1)}, bf16[4096,128]{1,0:T(8,128)(2,1)}, u32[]{:S(2)}) copy-start(bf16[4096,128]{1,0:T(8,128)(2,1)} %param.14) | copy-start | bytes 3145732
  7.2 320.1 %all-reduce.3.cloned.1.call-start = ((), (), s32[]{:S(2)}) async-start(), calls=%async_computation | async-start | bytes 917504 | tf_op jit(solution)/shard_map/psum | solution.py:151
  8.1 11.3 %collective-permute-start.1 = (bf16[1,1,32,128]{3,2,1,0:T(8,128)(2,1)S(1)}, bf16[1,1,32,128]{3,2,1,0:T(8,128)(2,1)S(1)}, u32[]{:S(2)}, u32[]{:S(2)}) collective-permute-start(bf16[1,1,32,128]{3,2,1,0:T(8,128)(2,1)S(1)} %slice_bitcast_fusion.6), channel_id=1, source_target_pairs={{32,0},{64,32},{96,64},{128,96},{160,128},{192,160},{224,192},{33,... | collective-permute-start | bytes 24584 | tf_op jit(solution)/shard_map/ppermute | solution.py:19
  13.2 6.2 %collective-permute-start = (bf16[1,1,32,128]{3,2,1,0:T(8,128)(2,1)S(1)}, bf16[1,1,32,128]{3,2,1,0:T(8,128)(2,1)S(1)}, u32[]{:S(2)}, u32[]{:S(2)}) collective-permute-start(bf16[1,1,32,128]{3,2,1,0:T(8,128)(2,1)S(1)} %slice_bitcast_fusion.6), channel_id=1, source_target_pairs={{0,32},{32,64},{64,96},{96,128},{128,160},{160,192},{192,224},{1,3... | collective-permute-start | bytes 24584 | tf_op jit(solution)/shard_map/ppermute | solution.py:16
  18.0 7.5 %copy-start.3 = (bf16[4096,128]{1,0:T(8,128)(2,1)S(1)}, bf16[4096,128]{1,0:T(8,128)(2,1)}, u32[]{:S(2)}) copy-start(bf16[4096,128]{1,0:T(8,128)(2,1)} %param.23) | copy-start | bytes 3145732
  19.4 6.7 %collective-permute-start.3 = (bf16[3,1,32,128]{3,2,1,0:T(8,128)(2,1)S(1)}, bf16[3,1,32,128]{3,2,1,0:T(8,128)(2,1)S(1)}, u32[]{:S(2)}, u32[]{:S(2)}) collective-permute-start(bf16[3,1,32,128]{3,2,1,0:T(8,128)(2,1)S(1)} %pad_maximum_fusion.7), channel_id=1, source_target_pairs={{1,0},{2,1},{3,2},{4,3},{5,4},{6,5},{7,6},{8,7},{9,8},{10,9},{11,1... | collective-permute-start | bytes 73736 | tf_op jit(solution)/shard_map/ppermute | solution.py:19
  20.7 5.4 %collective-permute-start.2 = (bf16[3,1,32,128]{3,2,1,0:T(8,128)(2,1)S(1)}, bf16[3,1,32,128]{3,2,1,0:T(8,128)(2,1)S(1)}, u32[]{:S(2)}, u32[]{:S(2)}) collective-permute-start(bf16[3,1,32,128]{3,2,1,0:T(8,128)(2,1)S(1)} %pad_maximum_fusion.7), channel_id=1, source_target_pairs={{0,1},{1,2},{2,3},{3,4},{4,5},{5,6},{6,7},{7,8},{8,9},{9,10},{10,1... | collective-permute-start | bytes 73736 | tf_op jit(solution)/shard_map/ppermute | solution.py:16
  26.1 2.9 copy-start.13
  29.0 1.6 copy-start.8
  30.6 0.8 copy-start.12
  31.4 2.0 copy-start.7
  31.4 2.2 copy-start.9
  34.5 2.6 copy-start.4
  41.6 1.0 copy-start.11
  42.6 4.5 %copy-start.1 = (f32[4096,384]{1,0:T(8,128)}, f32[4096,384]{1,0:T(8,128)S(1)}, u32[]{:S(2)}) copy-start(f32[4096,384]{1,0:T(8,128)S(1)} %fusion.71) | copy-start | bytes 18874372
  42.6 4.6 %slice-start = ((f32[256,256]{1,0:T(8,128)}), f32[256,128]{1,0:T(8,128)S(1)}, s32[]{:S(2)}) async-start(f32[256,256]{1,0:T(8,128)} %copy-done.4), calls=%async_computation.1 | async-start | bytes 262144 | tf_op jit(solution)/shard_map/slice | solution.py:140
  47.7 10.1 %collective-permute-start.4 = (bf16[3,32,128]{1,2,0:T(8,128)(2,1)S(1)}, bf16[3,32,128]{1,2,0:T(8,128)(2,1)S(1)}, u32[]{:S(2)}, u32[]{:S(2)}) collective-permute-start(bf16[3,32,128]{1,2,0:T(8,128)(2,1)S(1)} %get-tuple-element.50), channel_id=1, source_target_pairs={{1,0},{2,1},{3,2},{4,3},{5,4},{6,5},{7,6},{8,7},{9,8},{10,9},{11,1... | collective-permute-start | bytes 73736 | tf_op jit(solution)/shard_map/ppermute | solution.py:27
  49.0 8.8 %collective-permute-start.5 = (bf16[3,32,128]{1,2,0:T(8,128)(2,1)S(1)}, bf16[3,32,128]{1,2,0:T(8,128)(2,1)S(1)}, u32[]{:S(2)}, u32[]{:S(2)}) collective-permute-start(bf16[3,32,128]{1,2,0:T(8,128)(2,1)S(1)} %get-tuple-element.51), channel_id=1, source_target_pairs={{0,1},{1,2},{2,3},{3,4},{4,5},{5,6},{6,7},{7,8},{8,9},{9,10},{10,1... | collective-permute-start | bytes 73736 | tf_op jit(solution)/shard_map/ppermute | solution.py:27
  57.8 8.8 %collective-permute-start.6 = (f32[32,128]{0,1:T(8,128)S(1)}, f32[32,128]{0,1:T(8,128)S(1)}, u32[]{:S(2)}, u32[]{:S(2)}) collective-permute-start(f32[32,128]{0,1:T(8,128)S(1)} %get-tuple-element.52), channel_id=1, source_target_pairs={{32,0},{64,32},{96,64},{128,96},{160,128},{192,160},{224,192},{33,... | collective-permute-start | bytes 49160 | tf_op jit(solution)/shard_map/ppermute | solution.py:27
  61.8 4.8 %collective-permute-start.7 = (f32[32,128]{0,1:T(8,128)S(1)}, f32[32,128]{0,1:T(8,128)S(1)}, u32[]{:S(2)}, u32[]{:S(2)}) collective-permute-start(f32[32,128]{0,1:T(8,128)S(1)} %get-tuple-element.53), channel_id=1, source_target_pairs={{0,32},{32,64},{64,96},{96,128},{128,160},{160,192},{192,224},{1,3... | collective-permute-start | bytes 49160 | tf_op jit(solution)/shard_map/ppermute | solution.py:27
Sparse Core Ops, SparseCore 0:
  66.7 260.5 all-reduce.2
where the time goes:
time: 341 us; the launch traced here: 340 us
  waiting for transfers between devices  259 us (76%)
  matrix products  28.1 us (8%)
  starting transfers between devices  23.5 us (7%)
  between operations  15.3 us (4%)
  other arithmetic  8.02 us (2%)
  local copies, waits for them, and re-layouts  6.07 us (2%)
    psum x1, waiting for transfers between devices, shards(): totals = lax.psum((ge_in, ge_out, gn_in, gn_out), ('strip', 'sub'))  259 us
    ppermute x4, starting transfers between devices, shifted(): lax.ppermute(value, axis, [(source, source + steps) for source in range(f...  11.1 us
    dot_general x3, matrix products, sum_rows(): jnp.dot(onehot.astype(jnp.float32).T, values, precision=lax.Precision.HIG...  10.4 us
  transfers between devices with their start and end apart: 9, of which 1 were waited for; matrix products, arithmetic and copies ran while one was open for 4% of the time, Pallas kernels for 0%

commit v1 on v0

v1 whole, which is shorter than its diff:
```python
import functools
import math

import jax
import jax.numpy as jnp
from jax import lax
from jax.experimental import pallas as pl
from jax.experimental.pallas import tpu as pltpu
from jax.sharding import PartitionSpec as P

EPS = 1e-05
MESH = pl.DeviceIdType.MESH
F32 = jnp.float32
BF16 = jnp.bfloat16

H = 128
CHUNK = 512
NEAR = [(ds, dj) for ds in (-1, 0, 1) for dj in (-1, 0, 1) if (ds, dj) != (0, 0)]


def dot(a, b):
    return lax.dot_general(a, b, (((1,), (0,)), ((), ())), preferred_element_type=F32)


def dot_nt(a, b):
    return lax.dot_general(a, b, (((1,), (1,)), ((), ())), preferred_element_type=F32)


def dot_tn(a, b):
    return lax.dot_general(a, b, (((0,), (0,)), ((), ())), preferred_element_type=F32)


def split(x):
    high = x.astype(BF16)
    return high, (x - high.astype(F32)).astype(BF16)


def silu_parts(z):
    half = 0.5 * z
    s = 0.5 + 0.5 * jnp.tanh(half)
    a = z * s
    return a, s + a - a * s


def mean_row(x):
    return jnp.mean(x, axis=1, keepdims=True)


def edge_kernel(
    place_ref,
    count_ref,
    nodes_ref,
    halo_ref,
    edges_ref,
    cot_ref,
    send_ref,
    recv_ref,
    w_ei_ref,
    w_eo_ref,
    w_ni_ref,
    w_no_ref,
    ncot_ref,
    new_nodes_ref,
    new_edges_ref,
    local_ref,
    owed_ref,
    grads_ref,
    table_ref,
    sidx_ref,
    weo_ref,
    hotr_ref,
    a1_ref,
    sp_ref,
    n2_ref,
    r2_ref,
    agg_ref,
    dagg_ref,
    gsum_ref,
):
    n_p = nodes_ref.shape[0]
    n_e = edges_ref.shape[0]
    n_h = halo_ref.shape[0]
    border = n_h // 8
    n_s = n_p + n_h
    rows = CHUNK // 128
    steps = n_e // CHUNK
    count = count_ref[0]

    owner = send_ref[...] // n_p
    within = send_ref[...] % n_p
    d_strip = owner // place_ref[2] - place_ref[0]
    d_sub = owner % place_ref[2] - place_ref[1]
    block = (d_strip + 1) * 3 + d_sub + 1
    slot = jnp.where(block > 4, block - 1, block)
    sidx_ref[...] = jnp.where(block == 4, within, n_p + slot * border + (within & (border - 1)))

    table_ref[0:n_p, :] = dot(nodes_ref[...], w_ei_ref[0:H, :]).astype(BF16)
    table_ref[n_p:n_s, :] = dot(halo_ref[...], w_ei_ref[0:H, :]).astype(BF16)
    table_ref[n_s : n_s + n_p, :] = dot(nodes_ref[...], w_ei_ref[H : 2 * H, :]).astype(BF16)
    table_ref[n_s + n_p :, :] = w_ei_ref[2 * H :, :]
    weo = w_eo_ref[...].astype(F32)
    high, low = split(weo - mean_row(weo))
    weo_ref[0:H, :] = high
    weo_ref[H:, :] = low
    agg_ref[...] = jnp.zeros_like(agg_ref)
    gsum_ref[...] = jnp.zeros_like(gsum_ref)

    lane = lax.broadcasted_iota(jnp.int32, (CHUNK, 128), 1)

    def column(ref, c):
        return jnp.concatenate(
            [
                jnp.broadcast_to(ref[pl.ds(c * rows + k, 1), :], (128, 128)).T
                for k in range(rows)
            ],
            axis=0,
        )

    def hot_rows(col, n):
        return jnp.concatenate(
            [(col == lane + k * 128).astype(F32).astype(BF16) for k in range(n // 128)], axis=1
        )

    def hot_cols(ref, c, n):
        sub = lax.broadcasted_iota(jnp.int32, (n, 128), 0)
        return jnp.concatenate(
            [
                (jnp.broadcast_to(ref[pl.ds(c * rows + k, 1), :], (n, 128)) == sub)
                .astype(F32)
                .astype(BF16)
                for k in range(rows)
            ],
            axis=1,
        )

    def forward(c, carry):
        at = pl.ds(pl.multiple_of(c * CHUNK, CHUNK), CHUNK)
        hot_s = hot_rows(column(sidx_ref, c), n_s)
        hot_r = hot_rows(column(recv_ref, c), n_p)
        hotr_ref[at, :] = hot_r
        edges = edges_ref[at, :]
        z1 = dot(jnp.concatenate([hot_s, hot_r, edges], axis=1), table_ref[...])
        a1, sp = silu_parts(z1)
        a1 = a1.astype(BF16)
        a1_ref[at, :] = a1
        sp_ref[at, :] = sp
        centre = dot(jnp.concatenate([a1, a1], axis=1), weo_ref[...])
        r2 = lax.rsqrt(mean_row(centre * centre) + EPS)
        where = c * CHUNK + lax.broadcasted_iota(jnp.int32, (CHUNK, 1), 0)
        r2 = jnp.where(where < count, r2, 0.0)
        n2 = centre * r2
        n2_ref[at, :] = n2
        r2_ref[at, :] = jnp.broadcast_to(r2, (CHUNK, 128))
        new_edges_ref[at, :] = (edges.astype(F32) + n2).astype(BF16)
        agg_ref[...] += dot(hot_cols(recv_ref, c, n_p), n2.astype(BF16))
        return carry

    lax.fori_loop(0, steps, forward, 0)

    nodes = nodes_ref[...]
    joined = jnp.concatenate([nodes, agg_ref[...].astype(BF16)], axis=1)
    a3, sp3 = silu_parts(dot(joined, w_ni_ref[...]))
    a3 = a3.astype(BF16)
    z4 = dot(a3, w_no_ref[...])
    centre = z4 - mean_row(z4)
    r4 = lax.rsqrt(mean_row(centre * centre) + EPS)
    n4 = centre * r4
    new_nodes_ref[...] = (nodes.astype(F32) + n4).astype(BF16)
    ncot = ncot_ref[...].astype(F32)
    dz4 = (r4 * (ncot - mean_row(ncot) - n4 * mean_row(ncot * n4))).astype(BF16)
    dz3 = (dot_nt(dz4, w_no_ref[...]) * sp3).astype(BF16)
    d_joined = dot_nt(dz3, w_ni_ref[...])
    dagg_ref[...] = d_joined[:, H:].astype(BF16)
    local_ref[...] = ncot + d_joined[:, :H]
    grads_ref[4 * H : 6 * H, :] = dot_tn(joined, dz3)
    grads_ref[6 * H : 7 * H, :] = dot_tn(a3, dz4)
    grads_ref[2 * H : 4 * H, :] = jnp.zeros((2 * H, H), F32)

    def backward(c, carry):
        at = pl.ds(pl.multiple_of(c * CHUNK, CHUNK), CHUNK)
        n2 = n2_ref[at, :]
        g = cot_ref[at, :].astype(F32) + dot(hotr_ref[at, :], dagg_ref[...])
        dz2 = (r2_ref[at, :] * (g - mean_row(g) - n2 * mean_row(g * n2))).astype(BF16)
        dz1 = (dot_nt(dz2, w_eo_ref[...]) * sp_ref[at, :]).astype(BF16)
        grads_ref[2 * H : 3 * H, :] += dot_tn(edges_ref[at, :], dz1)
        grads_ref[3 * H : 4 * H, :] += dot_tn(a1_ref[at, :], dz2)
        hot = jnp.concatenate([hot_cols(sidx_ref, c, n_s), hot_cols(recv_ref, c, n_p)], axis=0)
        gsum_ref[...] += dot(hot, dz1)
        return carry

    lax.fori_loop(0, steps, backward, 0)

    g_s = gsum_ref[0:n_s, :].astype(BF16)
    g_r = gsum_ref[n_s:, :].astype(BF16)
    w_s, w_r = w_ei_ref[0:H, :], w_ei_ref[H : 2 * H, :]
    grads_ref[0:H, :] = dot_tn(nodes, g_s[0:n_p, :]) + dot_tn(halo_ref[...], g_s[n_p:, :])
    grads_ref[H : 2 * H, :] = dot_tn(nodes, g_r)
    local_ref[...] += dot_nt(g_s[0:n_p, :], w_s) + dot_nt(g_r, w_r)
    owed_ref[...] = dot_nt(g_s[n_p:, :], w_s).astype(BF16)


def vmem():
    return pl.BlockSpec(memory_space=pltpu.VMEM)


def smem():
    return pl.BlockSpec(memory_space=pltpu.SMEM)


def edge_call(place, count, nodes, halo, edges, cot, send, recv, w_ei, w_eo, w_ni, w_no, ncot):
    n_p, n_h, n_e = nodes.shape[0], halo.shape[0], edges.shape[0]
    n_s = n_p + n_h
    send = send.reshape(n_e // 128, 128)
    recv = recv.reshape(n_e // 128, 128)
    return pl.pallas_call(
        edge_kernel,
        out_shape=(
            jax.ShapeDtypeStruct((n_p, H), BF16),
            jax.ShapeDtypeStruct((n_e, H), BF16),
            jax.ShapeDtypeStruct((n_p, H), F32),
            jax.ShapeDtypeStruct((n_h, H), BF16),
            jax.ShapeDtypeStruct((7 * H, H), F32),
        ),
        in_specs=[smem(), smem()] + [vmem()] * 11,
        out_specs=[vmem()] * 5,
        scratch_shapes=[
            pltpu.VMEM((n_s + n_p + H, H), BF16),
            pltpu.VMEM((n_e // 128, 128), jnp.int32),
            pltpu.VMEM((2 * H, H), BF16),
            pltpu.VMEM((n_e, n_p), BF16),
            pltpu.VMEM((n_e, H), BF16),
            pltpu.VMEM((n_e, H), F32),
            pltpu.VMEM((n_e, H), F32),
            pltpu.VMEM((n_e, H), F32),
            pltpu.VMEM((n_p, H), F32),
            pltpu.VMEM((n_p, H), BF16),
            pltpu.VMEM((n_s + n_p, H), F32),
        ],
        compiler_params=pltpu.CompilerParams(vmem_limit_bytes=48 << 20),
    )(place, count, nodes, halo, edges, cot, send, recv, w_ei, w_eo, w_ni, w_no, ncot)


def around(size_strip, size_sub):
    strip, sub = lax.axis_index("strip"), lax.axis_index("sub")
    return [
        (lax.rem(strip + ds + size_strip, size_strip), lax.rem(sub + dj + size_sub, size_sub))
        for ds, dj in NEAR
    ]


def swap_near(near, pieces, landing, send_sem, recv_sem):
    copies = []
    for k, peer in enumerate(near):
        copies.append(
            pltpu.make_async_remote_copy(
                src_ref=pieces[k],
                dst_ref=landing.at[7 - k],
                send_sem=send_sem.at[k],
                recv_sem=recv_sem.at[7 - k],
                device_id=peer,
                device_id_type=MESH,
            )
        )
    return copies


def greet(peers):
    barrier = pltpu.get_barrier_semaphore()
    for peer in peers:
        pl.semaphore_signal(barrier, inc=1, device_id=peer, device_id_type=MESH)
    pl.semaphore_wait(barrier, len(peers))


def halo_kernel(sizes, rim_ref, out_ref, landing, send_sem, recv_sem):
    near = around(*sizes)
    greet(near)
    copies = swap_near(near, [rim_ref] * 8, landing, send_sem, recv_sem)
    for copy in copies:
        copy.start()
    for copy in copies:
        copy.wait()
    for k in range(8):
        out_ref[k] = landing[k]


def halo_call(sizes, rim):
    border, width = rim.shape
    return pl.pallas_call(
        functools.partial(halo_kernel, sizes),
        out_shape=jax.ShapeDtypeStruct((8, border, width), BF16),
        in_specs=[vmem()],
        out_specs=vmem(),
        scratch_shapes=[
            pltpu.VMEM((8, border, width), BF16),
            pltpu.SemaphoreType.DMA((8,)),
            pltpu.SemaphoreType.DMA((8,)),
        ],
        compiler_params=pltpu.CompilerParams(collective_id=0, has_side_effects=True),
    )(rim)


def total_kernel(
    sizes,
    factor,
    local_ref,
    owed_ref,
    part_ref,
    node_grad_ref,
    total_ref,
    near_land,
    near_send,
    near_recv,
    c_out,
    c_land,
    x_out,
    x_land,
    y_out,
    y_land,
    z_out,
    z_land,
    y_all,
    x_all,
    c_all,
    send_sem,
    recv_sem,
):
    strip, sub = lax.axis_index("strip"), lax.axis_index("sub")
    my_x, my_c = strip // 2, strip % 2
    my_z, my_y = sub // 4, sub % 4
    near = around(*sizes)
    mate = (my_x * 2 + 1 - my_c, sub)
    row_x = [(lax.rem(my_x + d, 4) * 2 + my_c, sub) for d in (1, 2, 3)]
    row_y = [(strip, my_z * 4 + lax.rem(my_y + d, 4)) for d in (1, 2, 3)]
    row_z = [(strip, lax.rem(my_z + d, 8) * 4 + my_y) for d in range(1, 8)]
    greet(near + [mate] + row_x + row_y + row_z)

    def send(src, dst, k, peer):
        copy = pltpu.make_async_remote_copy(
            src_ref=src,
            dst_ref=dst,
            send_sem=send_sem.at[k],
            recv_sem=recv_sem.at[k],
            device_id=peer,
            device_id_type=MESH,
        )
        copy.start()
        return copy

    half = 448
    c_out[...] = part_ref[pl.ds((1 - my_c) * half, half), :].astype(BF16)
    core = send(c_out, c_land, 0, mate)
    returned = swap_near(
        near, [owed_ref.at[k] for k in range(8)], near_land, near_send, near_recv
    )
    for copy in returned:
        copy.start()
    mine = part_ref[pl.ds(my_c * half, half), :]
    core.wait()
    acc = mine + c_land[...].astype(F32)

    x_out[...] = acc.reshape(4, 112, H).astype(BF16)
    copies = [
        send(x_out.at[lax.rem(my_x + d, 4)], x_land.at[d - 1], d, row_x[d - 1]) for d in (1, 2, 3)
    ]
    for copy in copies:
        copy.wait()
    acc = x_out[my_x].astype(F32)
    for d in range(3):
        acc = acc + x_land[d].astype(F32)

    for k in range(4):
        low, high = 32 * k, min(32 * k + 32, 112)
        y_out[k, 0 : high - low, :] = acc[low:high, :].astype(BF16)
    y_out[3, 16:32, :] = jnp.zeros((16, H), BF16)
    copies = [
        send(y_out.at[lax.rem(my_y + d, 4)], y_land.at[d - 1], 3 + d, row_y[d - 1])
        for d in (1, 2, 3)
    ]
    for copy in copies:
        copy.wait()
    acc = y_out[my_y].astype(F32)
    for d in range(3):
        acc = acc + y_land[d].astype(F32)

    z_out[...] = acc.astype(BF16)
    copies = [send(z_out, z_land.at[my_z], 6 + d, row_z[d - 1]) for d in range(1, 8)]
    z_land[my_z] = z_out[...]
    for copy in copies:
        copy.wait()
    acc = z_land[0].astype(F32)
    for k in range(1, 8):
        acc = acc + z_land[k].astype(F32)

    y_all[my_y] = acc.astype(BF16)
    copies = [send(y_all.at[my_y], y_all.at[my_y], 13 + d, row_y[d - 1]) for d in (1, 2, 3)]
    for copy in copies:
        copy.wait()
    x_all[my_x] = y_all[...].reshape(128, H)[0:112, :]
    copies = [send(x_all.at[my_x], x_all.at[my_x], 16 + d, row_x[d - 1]) for d in (1, 2, 3)]
    for copy in copies:
        copy.wait()
    c_all[my_c] = x_all[...].reshape(half, H)
    core = send(c_all.at[my_c], c_all.at[my_c], 20, mate)
    core.wait()
    total_ref[...] = c_all[...].reshape(2 * half, H).astype(F32) * factor

    for copy in returned:
        copy.wait()
    back = near_land[0].astype(F32)
    for k in range(1, 8):
        back = back + near_land[k].astype(F32)
    border = back.shape[0]
    node_grad_ref[...] = local_ref[...]
    node_grad_ref[0:border, :] += back


def total_call(sizes, factor, local, owed, part):
    border = owed.shape[1]
    return pl.pallas_call(
        functools.partial(total_kernel, sizes, factor),
        out_shape=(
            jax.ShapeDtypeStruct(local.shape, F32),
            jax.ShapeDtypeStruct(part.shape, F32),
        ),
        in_specs=[vmem()] * 3,
        out_specs=[vmem()] * 2,
        scratch_shapes=[
            pltpu.VMEM((8, border, H), BF16),
            pltpu.SemaphoreType.DMA((8,)),
            pltpu.SemaphoreType.DMA((8,)),
            pltpu.VMEM((448, H), BF16),
            pltpu.VMEM((448, H), BF16),
            pltpu.VMEM((4, 112, H), BF16),
            pltpu.VMEM((3, 112, H), BF16),
            pltpu.VMEM((4, 32, H), BF16),
            pltpu.VMEM((3, 32, H), BF16),
            pltpu.VMEM((32, H), BF16),
            pltpu.VMEM((8, 32, H), BF16),
            pltpu.VMEM((4, 32, H), BF16),
            pltpu.VMEM((4, 112, H), BF16),
            pltpu.VMEM((2, 448, H), BF16),
            pltpu.SemaphoreType.DMA((21,)),
            pltpu.SemaphoreType.DMA((21,)),
        ],
        compiler_params=pltpu.CompilerParams(collective_id=1, has_side_effects=True),
    )(local, owed, part)


def shards(
    node_latents,
    edge_latents,
    senders,
    receivers,
    edge_count,
    w_edge_in,
    w_edge_out,
    w_node_in,
    w_node_out,
    node_cotangent,
    edge_cotangent,
):
    count_p = node_latents.shape[0]
    count_e = edge_latents.shape[0]
    border = count_p // 8
    sizes = (lax.axis_size("strip"), lax.axis_size("sub"))
    factor = 1.0 / math.sqrt(count_e * sizes[0] * sizes[1])
    place = jnp.stack(
        [lax.axis_index("strip"), lax.axis_index("sub"), jnp.int32(sizes[1])]
    ).astype(jnp.int32)
    halo = halo_call(sizes, node_latents[:border])
    new_nodes, new_edges, local, owed, part = edge_call(
        place,
        edge_count,
        node_latents,
        halo.reshape(8 * border, H),
        edge_latents,
        edge_cotangent,
        senders,
        receivers,
        w_edge_in,
        w_edge_out,
        w_node_in,
        w_node_out,
        node_cotangent,
    )
    node_grad, total = total_call(sizes, factor, local, owed.reshape(8, border, H), part)
    return (
        new_nodes,
        new_edges,
        node_grad,
        total[: 3 * H],
        total[3 * H : 4 * H],
        total[4 * H : 6 * H],
        total[6 * H :],
    )


def solution(mesh):
    placed = (
        P(("strip", "sub"), None),
        P(("strip", "sub"), None),
        P(("strip", "sub")),
        P(("strip", "sub")),
        P(("strip", "sub")),
        P(),
        P(),
        P(),
        P(),
        P(("strip", "sub"), None),
        P(("strip", "sub"), None),
    )
    return jax.shard_map(
        shards,
        mesh=mesh,
        in_specs=placed,
        out_specs=(
            P(("strip", "sub"), None),
            P(("strip", "sub"), None),
            P(("strip", "sub"), None),
            P(),
            P(),
            P(),
            P(),
        ),
        check_vma=False,
    )
```

time: 341 us -> 80.5 us (0.24)
  waiting for transfers between devices: 259 us -> 0 us
  Pallas kernels: 0 us -> 61.5 us
  matrix products: 28.1 us -> 0 us
  starting transfers between devices: 23.5 us -> 0 us
  between operations: 15.3 us -> 1.38 us
  local copies, waits for them, and re-layouts: 6.07 us -> 16.8 us
  other arithmetic: 8.02 us -> 0.08 us
    psum x1 -> x0, waiting for transfers between devices: 259 us -> none  [shards(): totals = lax.psum((ge_in, ge_out, gn_in, gn_out), ('strip', 'sub'))]
    pallas_call x0 -> x3, Pallas kernels: none -> 61.5 us  [the longest x1 29.2 us: total_call(): pl.pallas_call(functools.partial(total_kernel, sizes, factor), out_shape=...]
    dot_general x18 -> x0, matrix products: 28.1 us -> none  [the longest x3 10.4 us: sum_rows(): jnp.dot(onehot.astype(jnp.float32).T, values, precision=lax.Precision.HIG...]
    ppermute x8 -> x0, starting transfers between devices: 23.4 us -> none  [the longest x4 11.1 us: shifted(): lax.ppermute(value, axis, [(source, source + steps) for source in range(f...]
    unnamed x37 -> x31, local copies, waits for them, and re-layouts: 4.33 us -> 10.8 us
    mul x4 -> x0, other arithmetic: 6.13 us -> none  [the longest x1 1.62 us: shards(): totals[0] * factor]
    slice x4, local copies, waits for them, and re-layouts: 0.03 us -> 6.04 us  [the longest x1 1.65 us: shards(): total[:3 * H]]
  transfers between devices with their start and end apart: 9 -> 0, of which waited for: 1 -> 0; matrix products, arithmetic and copies ran while one was open for 4% -> 0% of each run, Pallas kernels for 0% -> 0%
where the time goes in v1:
time: 80.5 us; the launch traced here: 79.8 us
  Pallas kernels  61.5 us (76%)
  local copies, waits for them, and re-layouts  16.8 us (21%)
  between operations  1.38 us (2%)
    pallas_call x1, Pallas kernels, total_call(): pl.pallas_call(functools.partial(total_kernel, sizes, factor), out_shape=...  29.2 us
    pallas_call x1, Pallas kernels, edge_call(): pl.pallas_call(edge_kernel, out_shape=(jax.ShapeDtypeStruct((n_p, H), BF1...  17.3 us
    pallas_call x1, Pallas kernels, halo_call(): pl.pallas_call(functools.partial(halo_kernel, sizes), out_shape=jax.Shape...  15.1 us
    unnamed x31, local copies, waits for them, and re-layouts  10.8 us
    slice x1, local copies, waits for them, and re-layouts, shards(): total[:3 * H]  1.65 us

profile of v1, /device:TPU:1, one launch (start us, length us, event | category | flops | bytes accessed | tf_op | source)
XLA Modules:
  0.0 79.8 jit_solution(10642940921596204702)
XLA Ops:
  0.6 0.0 copy-start.5
  1.3 0.1 pad_add_fusion.place_ref
  1.4 1.3 %slice.15.rim_ref = bf16[32,128]{1,0:T(8,128)(2,1)} slice(bf16[256,128]{1,0:T(8,128)(2,1)} %nodes_ref.1), slice={[0:32], [0:128]} | slice | bytes 16384 | tf_op jit(solution)/shard_map/slice | solution.py:470
  2.7 15.1 %shard_map.162 = bf16[8,32,128]{2,1,0:T(8,128)(2,1)} custom-call(bf16[32,128]{1,0:T(8,128)(2,1)} %slice.15.rim_ref), custom_call_target="tpu_custom_call" | custom-call | tf_op jit(solution)/shard_map/pallas_call | solution.py:288
  17.8 0.0 copy-done.5
  17.8 0.0 copy-start
  17.8 1.2 %copy-done = bf16[4096,128]{1,0:T(8,128)(2,1)S(1)} copy-done((bf16[4096,128]{1,0:T(8,128)(2,1)S(1)}, bf16[4096,128]{1,0:T(8,128)(2,1)}, u32[]{:S(2)}) %copy-start) | copy-done | bytes 1048600
  19.0 1.2 %copy-done.1 = bf16[4096,128]{1,0:T(8,128)(2,1)S(1)} copy-done((bf16[4096,128]{1,0:T(8,128)(2,1)S(1)}, bf16[4096,128]{1,0:T(8,128)(2,1)}, u32[]{:S(2)}) %copy-start.1) | copy-done | bytes 1048600
  20.2 0.8 %copy-done.3 = bf16[8,32,128]{2,1,0:T(8,128)(2,1)S(1)} copy-done((bf16[8,32,128]{2,1,0:T(8,128)(2,1)S(1)}, bf16[8,32,128]{2,1,0:T(8,128)(2,1)}, u32[]{:S(2)}) %copy-start.3) | copy-done | bytes 65560
  21.1 0.8 %copy-done.6 = bf16[256,128]{1,0:T(8,128)(2,1)S(1)} copy-done((bf16[256,128]{1,0:T(8,128)(2,1)S(1)}, bf16[256,128]{1,0:T(8,128)(2,1)}, u32[]{:S(2)}) %copy-start.6) | copy-done | bytes 65560
  21.9 0.8 %copy-done.7 = bf16[256,128]{1,0:T(8,128)(2,1)S(1)} copy-done((bf16[256,128]{1,0:T(8,128)(2,1)S(1)}, bf16[256,128]{1,0:T(8,128)(2,1)}, u32[]{:S(2)}) %copy-start.7) | copy-done | bytes 65560
  22.8 0.8 %copy-done.8 = bf16[256,128]{1,0:T(8,128)(2,1)S(1)} copy-done((bf16[256,128]{1,0:T(8,128)(2,1)S(1)}, bf16[256,128]{1,0:T(8,128)(2,1)}, u32[]{:S(2)}) %copy-start.8) | copy-done | bytes 65560
  23.6 0.8 copy-done.10
  24.4 0.8 copy-done.11
  25.1 0.7 copy-done.13
  25.8 17.3 %shard_map.163 = (bf16[256,128]{1,0:T(8,128)(2,1)}, bf16[4096,128]{1,0:T(8,128)(2,1)}, f32[256,128]{1,0:T(8,128)S(1)}, bf16[256,128]{1,0:T(8,128)(2,1)S(1)}, f32[896,128]{1,0:T(8,128)S(1)}) custom-call(s32[3]{0:T(128)S(1)} %pad_add_fusion.place_ref, s32[1]{0:T(128)S(6)} %copy.19.count_ref, bf16[256,128]{1,0:T(8,128)(2,1)S(1)} %copy-done.6, ...), custom_call_target="tpu_custom_call" | custom-call | tf_op jit(solution)/shard_map/pallas_call | solution.py:215
  43.1 0.8 copy-done.2
  43.9 0.7 copy-done.4
  44.5 0.6 copy-done.9
  45.1 29.2 %shard_map.164 = (f32[256,128]{1,0:T(8,128)}, f32[896,128]{1,0:T(8,128)}) custom-call(f32[256,128]{1,0:T(8,128)} %copy-done.4, bf16[8,32,128]{2,1,0:T(8,128)(2,1)} %bitcast.7, f32[896,128]{1,0:T(8,128)} %copy-done.2), custom_call_target="tpu_custom_call" | custom-call | tf_op jit(solution)/shard_map/pallas_call | solution.py:419
  74.4 1.6 %slice.18 = f32[256,128]{1,0:T(8,128)} slice(f32[896,128]{1,0:T(8,128)} %get-tuple-element.20), slice={[512:768], [0:128]} | slice | bytes 262144 | tf_op jit(solution)/shard_map/slice | solution.py:493
  76.0 1.5 %fusion = (f32[128,128]{1,0:T(8,128)}, f32[128,128]{1,0:T(8,128)}) fusion(f32[896,128]{1,0:T(8,128)} %get-tuple-element.20), kind=kLoop, calls=%fused_computation.1 | loop fusion | bytes 262144 | tf_op jit(solution)/shard_map/slice | solution.py:494
  77.5 1.7 %slice.16 = f32[384,128]{1,0:T(8,128)} slice(f32[896,128]{1,0:T(8,128)} %get-tuple-element.20), slice={[0:384], [0:128]} | slice | bytes 393216 | tf_op jit(solution)/shard_map/slice | solution.py:491
  79.1 0.7 copy.20
  (15 shorter events, 0.0 us)
Async XLA Ops:
  0.6 17.1 %copy-start.5 = (bf16[384,128]{1,0:T(8,128)(2,1)S(1)}, bf16[384,128]{1,0:T(8,128)(2,1)}, u32[]{:S(2)}) copy-start(bf16[384,128]{1,0:T(8,128)(2,1)} %w_ei_ref.1) | copy-start | bytes 294916
  2.7 15.1 %copy-start.12 = (s32[4096]{0:T(1024)S(1)}, s32[4096]{0:T(1024)}, u32[]{:S(2)}) copy-start(s32[4096]{0:T(1024)} %param.13) | copy-start | bytes 49156
  17.8 1.2 %copy-start = (bf16[4096,128]{1,0:T(8,128)(2,1)S(1)}, bf16[4096,128]{1,0:T(8,128)(2,1)}, u32[]{:S(2)}) copy-start(bf16[4096,128]{1,0:T(8,128)(2,1)} %edges_ref.1) | copy-start | bytes 3145732
  19.0 1.2 %copy-start.1 = (bf16[4096,128]{1,0:T(8,128)(2,1)S(1)}, bf16[4096,128]{1,0:T(8,128)(2,1)}, u32[]{:S(2)}) copy-start(bf16[4096,128]{1,0:T(8,128)(2,1)} %cot_ref.1) | copy-start | bytes 3145732
  20.2 0.8 %copy-start.3 = (bf16[8,32,128]{2,1,0:T(8,128)(2,1)S(1)}, bf16[8,32,128]{2,1,0:T(8,128)(2,1)}, u32[]{:S(2)}) copy-start(bf16[8,32,128]{2,1,0:T(8,128)(2,1)} %shard_map.162) | copy-start | bytes 196612
  21.1 0.8 %copy-start.6 = (bf16[256,128]{1,0:T(8,128)(2,1)S(1)}, bf16[256,128]{1,0:T(8,128)(2,1)}, u32[]{:S(2)}) copy-start(bf16[256,128]{1,0:T(8,128)(2,1)} %nodes_ref.1) | copy-start | bytes 196612
  21.9 0.8 %copy-start.7 = (bf16[256,128]{1,0:T(8,128)(2,1)S(1)}, bf16[256,128]{1,0:T(8,128)(2,1)}, u32[]{:S(2)}) copy-start(bf16[256,128]{1,0:T(8,128)(2,1)} %w_ni_ref.1) | copy-start | bytes 196612
  22.8 0.8 %copy-start.8 = (bf16[256,128]{1,0:T(8,128)(2,1)S(1)}, bf16[256,128]{1,0:T(8,128)(2,1)}, u32[]{:S(2)}) copy-start(bf16[256,128]{1,0:T(8,128)(2,1)} %ncot_ref.1) | copy-start | bytes 196612
  23.6 0.8 copy-start.10
  24.4 0.8 copy-start.11
  25.1 0.7 copy-start.13
  43.1 0.8 copy-start.2
  43.9 0.7 copy-start.4
  44.5 0.6 copy-start.9
  77.5 1.7 %copy-start.14 = (f32[256,128]{1,0:T(8,128)S(1)}, f32[256,128]{1,0:T(8,128)}, u32[]{:S(2)}) copy-start(f32[256,128]{1,0:T(8,128)} %get-tuple-element.32) | copy-start | bytes 393220

commit v2 on v0

v2 whole, which is shorter than its diff:
```python
import functools
import math

import jax
import jax.numpy as jnp
from jax import lax
from jax.experimental import pallas as pl
from jax.experimental.pallas import tpu as pltpu
from jax.sharding import PartitionSpec as P

EPS = 1e-05
MESH = pl.DeviceIdType.MESH
F32 = jnp.float32
BF16 = jnp.bfloat16

H = 128
CHUNK = 2048
WIDE = 2048
NEAR = [(ds, dj) for ds in (-1, 0, 1) for dj in (-1, 0, 1) if (ds, dj) != (0, 0)]


def dot(a, b):
    return lax.dot_general(a, b, (((1,), (0,)), ((), ())), preferred_element_type=F32)


def dot_nt(a, b):
    return lax.dot_general(a, b, (((1,), (1,)), ((), ())), preferred_element_type=F32)


def dot_tn(a, b):
    return lax.dot_general(a, b, (((0,), (0,)), ((), ())), preferred_element_type=F32)


def split(x):
    high = x.astype(BF16)
    return high, (x - high.astype(F32)).astype(BF16)


def silu_parts(z):
    half = 0.5 * z
    s = 0.5 + 0.5 * jnp.tanh(half)
    a = z * s
    return a, s + a - a * s


def mean_row(x):
    return jnp.mean(x, axis=1, keepdims=True)


def around(sizes):
    strip, sub = lax.axis_index("strip"), lax.axis_index("sub")
    return [
        (lax.rem(strip + ds + sizes[0], sizes[0]), lax.rem(sub + dj + sizes[1], sizes[1]))
        for ds, dj in NEAR
    ]


def remote(src, dst, send_sem, recv_sem, peer):
    return pltpu.make_async_remote_copy(
        src_ref=src,
        dst_ref=dst,
        send_sem=send_sem,
        recv_sem=recv_sem,
        device_id=peer,
        device_id_type=MESH,
    )


def step_kernel(
    sizes,
    nodes_hbm,
    edges_hbm,
    send_hbm,
    recv_hbm,
    count_hbm,
    w_ei_hbm,
    w_eo_hbm,
    w_ni_hbm,
    w_no_hbm,
    ncot_hbm,
    cot_hbm,
    new_nodes_hbm,
    new_edges_hbm,
    node_grad_hbm,
    total_hbm,
    nodes_ref,
    edges_ref,
    send_ref,
    recv_ref,
    count_ref,
    w_ei_ref,
    w_eo_ref,
    w_ni_ref,
    w_no_ref,
    ncot_ref,
    cot_ref,
    load_sem,
    new_nodes_ref,
    new_edges_ref,
    node_grad_ref,
    store_sem,
    halo_ref,
    owed_ref,
    back_ref,
    near_sem,
    table_ref,
    sidx_ref,
    weo_ref,
    hot_ref,
    z1_ref,
    a1_ref,
    sp_ref,
    n2_ref,
    r2_ref,
    agg_ref,
    dagg_ref,
    gsum_ref,
    part_ref,
    c_out,
    c_land,
    x_out,
    x_land,
    y_out,
    y_land,
    z_out,
    z_land,
    y_all,
    x_all,
    c_all,
    send_sem,
    recv_sem,
):
    n_p = nodes_ref.shape[0]
    n_e = edges_ref.shape[0]
    border = halo_ref.shape[1]
    n_h = 8 * border
    n_l = 2 * n_p + H
    strip, sub = lax.axis_index("strip"), lax.axis_index("sub")
    my_x, my_c = strip // 2, strip % 2
    my_z, my_y = sub // 4, sub % 4
    near = around(sizes)
    mate = (my_x * 2 + 1 - my_c, sub)
    row_x = [(lax.rem(my_x + d, 4) * 2 + my_c, sub) for d in (1, 2, 3)]
    row_y = [(strip, my_z * 4 + lax.rem(my_y + d, 4)) for d in (1, 2, 3)]
    row_z = [(strip, lax.rem(my_z + d, 8) * 4 + my_y) for d in range(1, 8)]
    peers = near + [mate] + row_x + row_y + row_z

    pairs = [
        (nodes_hbm, nodes_ref),
        (w_ei_hbm, w_ei_ref),
        (send_hbm, send_ref),
        (recv_hbm, recv_ref),
        (w_eo_hbm, w_eo_ref),
        (edges_hbm, edges_ref),
        (count_hbm, count_ref),
        (w_ni_hbm, w_ni_ref),
        (w_no_hbm, w_no_ref),
        (ncot_hbm, ncot_ref),
        (cot_hbm, cot_ref),
    ]
    loads = [pltpu.make_async_copy(a, b, load_sem.at[k]) for k, (a, b) in enumerate(pairs)]
    for load in loads:
        load.start()
    barrier = pltpu.get_barrier_semaphore()
    for peer in peers:
        pl.semaphore_signal(barrier, inc=1, device_id=peer, device_id_type=MESH)

    loads[0].wait()
    loads[1].wait()
    nodes = nodes_ref[...]
    table_ref[0:n_p, :] = dot(nodes, w_ei_ref[0:H, :]).astype(BF16)
    table_ref[n_p : 2 * n_p, :] = dot(nodes, w_ei_ref[H : 2 * H, :]).astype(BF16)
    table_ref[2 * n_p : n_l, :] = w_ei_ref[2 * H :, :]

    loads[2].wait()
    owner = send_ref[...] // n_p
    within = send_ref[...] % n_p
    d_strip = owner // sizes[1] - strip
    d_sub = owner % sizes[1] - sub
    block = (d_strip + 1) * 3 + d_sub + 1
    slot = jnp.where(block > 4, block - 1, block)
    sidx_ref[...] = jnp.where(block == 4, within, n_p + slot * border + (within & (border - 1)))
    loads[4].wait()
    weo = w_eo_ref[...].astype(F32)
    high, low = split(weo - mean_row(weo))
    weo_ref[0:H, :] = high
    weo_ref[H:, :] = low
    agg_ref[...] = jnp.zeros_like(agg_ref)
    gsum_ref[...] = jnp.zeros_like(gsum_ref)
    part_ref[2 * H : 4 * H, :] = jnp.zeros((2 * H, H), F32)

    pl.semaphore_wait(barrier, len(peers))
    halo_copies = [
        remote(
            nodes_ref.at[pl.ds(0, border), :],
            halo_ref.at[7 - k],
            near_sem.at[0, k],
            near_sem.at[1, 7 - k],
            peer,
        )
        for k, peer in enumerate(near)
    ]
    for copy in halo_copies:
        copy.start()

    def column(ref, c, size):
        rows = size // 128
        return jnp.concatenate(
            [
                jnp.broadcast_to(ref[pl.ds(c * rows + k, 1), :], (128, 128)).T.astype(jnp.int16)
                for k in range(rows)
            ],
            axis=0,
        )

    def hot_rows(col, first, n):
        size = col.shape[0]
        lane = lax.broadcasted_iota(jnp.int32, (size, 128), 1).astype(jnp.int16)
        one, zero = jnp.ones((size, 128), BF16), jnp.zeros((size, 128), BF16)
        return [
            jnp.where(col == lane + jnp.int16(first + k * 128), one, zero)
            for k in range(n // 128)
        ]

    def hot_cols(ref, c, size, n):
        rows = size // 128
        down = lax.broadcasted_iota(jnp.int32, (n, 128), 0).astype(jnp.int16)
        one, zero = jnp.ones((n, 128), BF16), jnp.zeros((n, 128), BF16)
        return jnp.concatenate(
            [
                jnp.where(
                    jnp.broadcast_to(ref[pl.ds(c * rows + k, 1), :], (n, 128)).astype(jnp.int16)
                    == down,
                    one,
                    zero,
                )
                for k in range(rows)
            ],
            axis=1,
        )

    loads[3].wait()
    loads[5].wait()

    def local_part(c, carry):
        at = pl.ds(pl.multiple_of(c * WIDE, WIDE), WIDE)
        col = column(sidx_ref, c, WIDE)
        hot_s = hot_rows(col, 0, n_p)
        hot_h = hot_rows(col, n_p, n_h)
        hot_r = hot_rows(column(recv_ref, c, WIDE), 0, n_p)
        hot_ref[at, :] = jnp.concatenate(hot_h + hot_r, axis=1)
        z1_ref[at, :] = dot(
            jnp.concatenate(hot_s + hot_r + [edges_ref[at, :]], axis=1), table_ref[0:n_l, :]
        )
        return carry

    lax.fori_loop(0, n_e // WIDE, local_part, 0)

    for copy in halo_copies:
        copy.wait()
    halo = halo_ref[...].reshape(n_h, H)
    table_ref[n_l:, :] = dot(halo, w_ei_ref[0:H, :]).astype(BF16)
    loads[6].wait()
    count = count_ref[0]

    def forward(c, carry):
        at = pl.ds(pl.multiple_of(c * CHUNK, CHUNK), CHUNK)
        z1 = z1_ref[at, :] + dot(hot_ref[at, 0:n_h], table_ref[n_l:, :])
        a1, sp = silu_parts(z1)
        a1 = a1.astype(BF16)
        a1_ref[at, :] = a1
        sp_ref[at, :] = sp
        centre = dot(jnp.concatenate([a1, a1], axis=1), weo_ref[...])
        r2 = lax.rsqrt(mean_row(centre * centre) + EPS)
        where = c * CHUNK + lax.broadcasted_iota(jnp.int32, (CHUNK, 1), 0)
        r2 = jnp.where(where < count, r2, 0.0)
        n2 = centre * r2
        n2_ref[at, :] = n2
        r2_ref[at, :] = jnp.broadcast_to(r2, (CHUNK, 128))
        new_edges_ref[at, :] = (edges_ref[at, :].astype(F32) + n2).astype(BF16)
        agg_ref[...] += dot(hot_cols(recv_ref, c, CHUNK, n_p), n2.astype(BF16))
        return carry

    lax.fori_loop(0, n_e // CHUNK, forward, 0)

    stores = [pltpu.make_async_copy(new_edges_ref, new_edges_hbm, store_sem.at[0])]
    stores[0].start()
    for k in (7, 8, 9):
        loads[k].wait()
    joined = jnp.concatenate([nodes, agg_ref[...].astype(BF16)], axis=1)
    a3, sp3 = silu_parts(dot(joined, w_ni_ref[...]))
    a3 = a3.astype(BF16)
    z4 = dot(a3, w_no_ref[...])
    centre = z4 - mean_row(z4)
    r4 = lax.rsqrt(mean_row(centre * centre) + EPS)
    n4 = centre * r4
    new_nodes_ref[...] = (nodes.astype(F32) + n4).astype(BF16)
    ncot = ncot_ref[...].astype(F32)
    dz4 = (r4 * (ncot - mean_row(ncot) - n4 * mean_row(ncot * n4))).astype(BF16)
    dz3 = (dot_nt(dz4, w_no_ref[...]) * sp3).astype(BF16)
    d_joined = dot_nt(dz3, w_ni_ref[...])
    dagg_ref[...] = d_joined[:, H:].astype(BF16)
    node_grad_ref[...] = ncot + d_joined[:, :H]
    part_ref[4 * H : 6 * H, :] = dot_tn(joined, dz3)
    part_ref[6 * H : 7 * H, :] = dot_tn(a3, dz4)
    stores.append(pltpu.make_async_copy(new_nodes_ref, new_nodes_hbm, store_sem.at[1]))
    stores[1].start()
    loads[10].wait()

    def backward(c, carry):
        at = pl.ds(pl.multiple_of(c * CHUNK, CHUNK), CHUNK)
        n2 = n2_ref[at, :]
        g = cot_ref[at, :].astype(F32) + dot(hot_ref[at, n_h:], dagg_ref[...])
        dz2 = (r2_ref[at, :] * (g - mean_row(g) - n2 * mean_row(g * n2))).astype(BF16)
        dz1 = (dot_nt(dz2, w_eo_ref[...]) * sp_ref[at, :]).astype(BF16)
        part_ref[2 * H : 3 * H, :] += dot_tn(edges_ref[at, :], dz1)
        part_ref[3 * H : 4 * H, :] += dot_tn(a1_ref[at, :], dz2)
        hot = jnp.concatenate(
            [hot_cols(sidx_ref, c, CHUNK, n_p + n_h), hot_cols(recv_ref, c, CHUNK, n_p)], axis=0
        )
        gsum_ref[...] += dot(hot, dz1)
        return carry

    lax.fori_loop(0, n_e // CHUNK, backward, 0)

    g_s = gsum_ref[0:n_p, :].astype(BF16)
    g_h = gsum_ref[n_p : n_p + n_h, :].astype(BF16)
    g_r = gsum_ref[n_p + n_h :, :].astype(BF16)
    w_s, w_r = w_ei_ref[0:H, :], w_ei_ref[H : 2 * H, :]
    part_ref[0:H, :] = dot_tn(nodes, g_s) + dot_tn(halo, g_h)
    part_ref[H : 2 * H, :] = dot_tn(nodes, g_r)

    half = c_out.shape[0]
    c_out[...] = part_ref[pl.ds((1 - my_c) * half, half), :].astype(BF16)
    core = remote(c_out, c_land, send_sem.at[0], recv_sem.at[0], mate)
    core.start()
    owed_ref[...] = dot_nt(g_h, w_s).astype(BF16).reshape(8, border, H)
    returned = [
        remote(owed_ref.at[k], back_ref.at[7 - k], near_sem.at[2, k], near_sem.at[3, 7 - k], peer)
        for k, peer in enumerate(near)
    ]
    for copy in returned:
        copy.start()
    node_grad_ref[...] += dot_nt(g_s, w_s) + dot_nt(g_r, w_r)
    mine = part_ref[pl.ds(my_c * half, half), :]
    core.wait()
    acc = mine + c_land[...].astype(F32)

    def share(src, dst, base, row):
        copies = [
            remote(src(d), dst(d), send_sem.at[base + d], recv_sem.at[base + d], peer)
            for d, peer in enumerate(row, 1)
        ]
        for copy in copies:
            copy.start()
        return copies

    piece = half // 4
    x_out[...] = acc.reshape(4, piece, H).astype(BF16)
    copies = share(lambda d: x_out.at[lax.rem(my_x + d, 4)], lambda d: x_land.at[d - 1], 0, row_x)
    for copy in copies:
        copy.wait()
    acc = x_out[my_x].astype(F32)
    for d in range(3):
        acc = acc + x_land[d].astype(F32)

    for k in range(4):
        low, high = 32 * k, min(32 * k + 32, piece)
        y_out[k, 0 : high - low, :] = acc[low:high, :].astype(BF16)
    y_out[3, 16:32, :] = jnp.zeros((16, H), BF16)
    copies = share(lambda d: y_out.at[lax.rem(my_y + d, 4)], lambda d: y_land.at[d - 1], 3, row_y)
    for copy in copies:
        copy.wait()
    acc = y_out[my_y].astype(F32)
    for d in range(3):
        acc = acc + y_land[d].astype(F32)

    z_out[...] = acc.astype(BF16)
    copies = share(lambda d: z_out, lambda d: z_land.at[my_z], 6, row_z)
    z_land[my_z] = z_out[...]

    for copy in returned:
        copy.wait()
    back = back_ref[0].astype(F32)
    for k in range(1, 8):
        back = back + back_ref[k].astype(F32)
    node_grad_ref[0:border, :] += back
    stores.append(pltpu.make_async_copy(node_grad_ref, node_grad_hbm, store_sem.at[2]))
    stores[2].start()

    for copy in copies:
        copy.wait()
    acc = z_land[0].astype(F32)
    for k in range(1, 8):
        acc = acc + z_land[k].astype(F32)

    y_all[my_y] = acc.astype(BF16)
    copies = share(lambda d: y_all.at[my_y], lambda d: y_all.at[my_y], 13, row_y)
    for copy in copies:
        copy.wait()
    x_all[my_x] = y_all[...].reshape(128, H)[0:piece, :]
    copies = share(lambda d: x_all.at[my_x], lambda d: x_all.at[my_x], 16, row_x)
    for copy in copies:
        copy.wait()
    c_all[my_c] = x_all[...].reshape(half, H)
    core = remote(c_all.at[my_c], c_all.at[my_c], send_sem.at[20], recv_sem.at[20], mate)
    core.start()
    core.wait()
    stores.append(pltpu.make_async_copy(c_all, total_hbm, store_sem.at[3]))
    stores[3].start()
    for store in stores:
        store.wait()


def vmem():
    return pl.BlockSpec(memory_space=pltpu.VMEM)


def hbm():
    return pl.BlockSpec(memory_space=pltpu.HBM)


def anywhere():
    return pl.BlockSpec(memory_space=pl.ANY)


def step_call(sizes, args):
    n_p, n_e = args[0].shape[0], args[1].shape[0]
    border = n_p // 8
    n_h = 8 * border
    half = 7 * H // 2
    dma = pltpu.SemaphoreType.DMA
    return pl.pallas_call(
        functools.partial(step_kernel, sizes),
        out_shape=(
            jax.ShapeDtypeStruct((n_p, H), BF16),
            jax.ShapeDtypeStruct((n_e, H), BF16),
            jax.ShapeDtypeStruct((n_p, H), F32),
            jax.ShapeDtypeStruct((2, half, H), BF16),
        ),
        in_specs=[hbm()] * 11,
        out_specs=[hbm()] * 4,
        scratch_shapes=[
            pltpu.SMEM(a.shape, a.dtype) if a.shape == (1,) else pltpu.VMEM(a.shape, a.dtype)
            for a in args
        ]
        + [
            dma((11,)),
            pltpu.VMEM((n_p, H), BF16),
            pltpu.VMEM((n_e, H), BF16),
            pltpu.VMEM((n_p, H), F32),
            dma((4,)),
            pltpu.VMEM((8, border, H), BF16),
            pltpu.VMEM((8, border, H), BF16),
            pltpu.VMEM((8, border, H), BF16),
            dma((4, 8)),
            pltpu.VMEM((2 * n_p + H + n_h, H), BF16),
            pltpu.VMEM((n_e // 128, 128), jnp.int32),
            pltpu.VMEM((2 * H, H), BF16),
            pltpu.VMEM((n_e, n_h + n_p), BF16),
            pltpu.VMEM((n_e, H), F32),
            pltpu.VMEM((n_e, H), BF16),
            pltpu.VMEM((n_e, H), F32),
            pltpu.VMEM((n_e, H), F32),
            pltpu.VMEM((n_e, H), F32),
            pltpu.VMEM((n_p, H), F32),
            pltpu.VMEM((n_p, H), BF16),
            pltpu.VMEM((2 * n_p + n_h, H), F32),
            pltpu.VMEM((7 * H, H), F32),
            pltpu.VMEM((half, H), BF16),
            pltpu.VMEM((half, H), BF16),
            pltpu.VMEM((4, half // 4, H), BF16),
            pltpu.VMEM((3, half // 4, H), BF16),
            pltpu.VMEM((4, 32, H), BF16),
            pltpu.VMEM((3, 32, H), BF16),
            pltpu.VMEM((32, H), BF16),
            pltpu.VMEM((8, 32, H), BF16),
            pltpu.VMEM((4, 32, H), BF16),
            pltpu.VMEM((4, half // 4, H), BF16),
            pltpu.VMEM((2, half, H), BF16),
            dma((21,)),
            dma((21,)),
        ],
        compiler_params=pltpu.CompilerParams(
            collective_id=0, has_side_effects=True, vmem_limit_bytes=62_000_000
        ),
    )(*args)


def finish_kernel(
    factor,
    nn_ref,
    ne_ref,
    ng_ref,
    total_ref,
    nn_out,
    ne_out,
    ng_out,
    ei_out,
    eo_out,
    ni_out,
    no_out,
    nn_buf,
    ne_buf,
    ng_buf,
    total_buf,
    grad_buf,
    in_sem,
    out_sem,
):
    quarter = ne_buf.shape[0] // 4
    parts = [pl.ds(k * quarter, quarter) for k in range(4)]
    brought = [pltpu.make_async_copy(total_ref, total_buf, in_sem.at[0])]
    for k, part in enumerate(parts):
        brought.append(
            pltpu.make_async_copy(ne_ref.at[part, :], ne_buf.at[part, :], in_sem.at[1 + k])
        )
    brought.append(pltpu.make_async_copy(ng_ref, ng_buf, in_sem.at[5]))
    brought.append(pltpu.make_async_copy(nn_ref, nn_buf, in_sem.at[6]))
    for copy in brought:
        copy.start()
    taken = []

    def take(src, dst):
        taken.append(pltpu.make_async_copy(src, dst, out_sem.at[len(taken)]))
        taken[-1].start()

    brought[0].wait()
    half = total_buf.shape[1]
    grad_buf[0:half, :] = total_buf[0].astype(F32) * factor
    grad_buf[half:, :] = total_buf[1].astype(F32) * factor
    first = 0
    for out in (ei_out, eo_out, ni_out, no_out):
        take(grad_buf.at[pl.ds(first, out.shape[0]), :], out)
        first += out.shape[0]
    for k, part in enumerate(parts):
        brought[1 + k].wait()
        take(ne_buf.at[part, :], ne_out.at[part, :])
    brought[5].wait()
    take(ng_buf, ng_out)
    brought[6].wait()
    take(nn_buf, nn_out)
    for copy in taken:
        copy.wait()


def finish_call(factor, new_nodes, new_edges, node_grad, total):
    shapes = [
        (new_nodes.shape, BF16),
        (new_edges.shape, BF16),
        (node_grad.shape, F32),
        ((3 * H, H), F32),
        ((H, H), F32),
        ((2 * H, H), F32),
        ((H, H), F32),
    ]
    return pl.pallas_call(
        functools.partial(finish_kernel, factor),
        out_shape=tuple(jax.ShapeDtypeStruct(s, t) for s, t in shapes),
        in_specs=[hbm()] * 4,
        out_specs=[hbm()] * 7,
        scratch_shapes=[
            pltpu.VMEM(new_nodes.shape, BF16),
            pltpu.VMEM(new_edges.shape, BF16),
            pltpu.VMEM(node_grad.shape, F32),
            pltpu.VMEM(total.shape, BF16),
            pltpu.VMEM((7 * H, H), F32),
            pltpu.SemaphoreType.DMA((7,)),
            pltpu.SemaphoreType.DMA((10,)),
        ],
        compiler_params=pltpu.CompilerParams(vmem_limit_bytes=62_000_000),
    )(new_nodes, new_edges, node_grad, total)


def shards(
    node_latents,
    edge_latents,
    senders,
    receivers,
    edge_count,
    w_edge_in,
    w_edge_out,
    w_node_in,
    w_node_out,
    node_cotangent,
    edge_cotangent,
):
    count_e = edge_latents.shape[0]
    sizes = (lax.axis_size("strip"), lax.axis_size("sub"))
    factor = 1.0 / math.sqrt(count_e * sizes[0] * sizes[1])
    return finish_call(
        factor,
        *step_call(
            sizes,
            (
                node_latents,
                edge_latents,
                senders.reshape(count_e // 128, 128),
                receivers.reshape(count_e // 128, 128),
                edge_count,
                w_edge_in,
                w_edge_out,
                w_node_in,
                w_node_out,
                node_cotangent,
                edge_cotangent,
            ),
        )
    )


def solution(mesh):
    placed = (
        P(("strip", "sub"), None),
        P(("strip", "sub"), None),
        P(("strip", "sub")),
        P(("strip", "sub")),
        P(("strip", "sub")),
        P(),
        P(),
        P(),
        P(),
        P(("strip", "sub"), None),
        P(("strip", "sub"), None),
    )
    return jax.shard_map(
        shards,
        mesh=mesh,
        in_specs=placed,
        out_specs=(
            P(("strip", "sub"), None),
            P(("strip", "sub"), None),
            P(("strip", "sub"), None),
            P(),
            P(),
            P(),
            P(),
        ),
        check_vma=False,
    )
```

time: 341 us -> 51 us (0.15)
  waiting for transfers between devices: 259 us -> 0 us
  Pallas kernels: 0 us -> 49.6 us
  matrix products: 28.1 us -> 0 us
  starting transfers between devices: 23.5 us -> 0 us
  between operations: 15.3 us -> 1.29 us
  other arithmetic: 8.02 us -> 0 us
  local copies, waits for them, and re-layouts: 6.07 us -> 0 us
    psum x1 -> x0, waiting for transfers between devices: 259 us -> none  [shards(): totals = lax.psum((ge_in, ge_out, gn_in, gn_out), ('strip', 'sub'))]
    pallas_call x0 -> x2, Pallas kernels: none -> 49.6 us  [the longest x1 47.3 us: step_call(): pl.pallas_call(functools.partial(step_kernel, sizes), out_shape=(jax.Shap...]
    dot_general x18 -> x0, matrix products: 28.1 us -> none  [the longest x3 10.4 us: sum_rows(): jnp.dot(onehot.astype(jnp.float32).T, values, precision=lax.Precision.HIG...]
    ppermute x8 -> x0, starting transfers between devices: 23.4 us -> none  [the longest x4 11.1 us: shifted(): lax.ppermute(value, axis, [(source, source + steps) for source in range(f...]
    mul x4 -> x0, other arithmetic: 6.13 us -> none  [the longest x1 1.62 us: shards(): totals[0] * factor]
    unnamed x37 -> x0, local copies, waits for them, and re-layouts: 4.33 us -> none
  transfers between devices with their start and end apart: 9 -> 0, of which waited for: 1 -> 0; matrix products, arithmetic and copies ran while one was open for 4% -> 0% of each run, Pallas kernels for 0% -> 0%
where the time goes in v2:
time: 51 us; the launch traced here: 50.9 us
  Pallas kernels  49.6 us (97%)
  between operations  1.29 us (3%)
    pallas_call x1, Pallas kernels, step_call(): pl.pallas_call(functools.partial(step_kernel, sizes), out_shape=(jax.Shap...  47.3 us
    pallas_call x1, Pallas kernels, finish_call(): pl.pallas_call(functools.partial(finish_kernel, factor), out_shape=tuple(...  2.29 us

profile of v2, /device:TPU:1, one launch (start us, length us, event | category | flops | bytes accessed | tf_op | source)
XLA Modules:
  0.0 50.9 jit_solution(3801792914904967331)
XLA Ops:
  1.3 47.3 %shard_map.162 = (bf16[256,128]{1,0:T(8,128)(2,1)}, bf16[4096,128]{1,0:T(8,128)(2,1)}, f32[256,128]{1,0:T(8,128)}, bf16[2,448,128]{2,1,0:T(8,128)(2,1)}) custom-call(bf16[256,128]{1,0:T(8,128)(2,1)} %nodes_hbm.1, bf16[4096,128]{1,0:T(8,128)(2,1)} %edges_hbm.1, s32[32,128]{1,0:T(8,128)} %bitcast.2, s32[32,128]{1,0:T(8,128)} %bitcast.3, s32[1]{0:T(128)S(6)} %copy.18.count_hbm, ...), custom_call_target="tpu_custom_call" | custom-call | tf_op jit(solution)/shard_map/pallas_call | solution.py:433
  48.6 2.3 %shard_map.163 = (bf16[256,128]{1,0:T(8,128)(2,1)}, bf16[4096,128]{1,0:T(8,128)(2,1)}, f32[256,128]{1,0:T(8,128)}, f32[384,128]{1,0:T(8,128)}, f32[128,128]{1,0:...) custom-call(bf16[256,128]{1,0:T(8,128)(2,1)} %get-tuple-element.11.nn_ref, bf16[4096,128]{1,0:T(8,128)(2,1)} %get-tuple-element.12.ne_ref, ...), custom_call_target="tpu_custom_call" | custom-call | tf_op jit(solution)/shard_map/pallas_call | solution.py:557

commit v3 on v2

--- a/solution.py
+++ b/solution.py
@@ -16,6 +16,9 @@
 H = 128
 CHUNK = 2048
 WIDE = 2048
+PIECES = [(112 * (k // 4) + 32 * (k % 4), 16 if k % 4 == 3 else 32) for k in range(16)]
+HOPS = [min(d // 4, 4 - d // 4) + min(d % 4, 4 - d % 4) for d in range(16)]
+FROM_NEAR = sorted(range(1, 16), key=lambda d: HOPS[d])
 NEAR = [(ds, dj) for ds in (-1, 0, 1) for dj in (-1, 0, 1) if (ds, dj) != (0, 0)]
 
 
@@ -118,15 +121,11 @@
     part_ref,
     c_out,
     c_land,
-    x_out,
-    x_land,
-    y_out,
-    y_land,
+    p_out,
+    p_land,
     z_out,
     z_land,
-    y_all,
-    x_all,
-    c_all,
+    all_ref,
     send_sem,
     recv_sem,
 ):
@@ -140,10 +139,15 @@
     my_z, my_y = sub // 4, sub % 4
     near = around(sizes)
     mate = (my_x * 2 + 1 - my_c, sub)
-    row_x = [(lax.rem(my_x + d, 4) * 2 + my_c, sub) for d in (1, 2, 3)]
-    row_y = [(strip, my_z * 4 + lax.rem(my_y + d, 4)) for d in (1, 2, 3)]
+
+    def shifted(dx, dy):
+        return lax.rem(my_x + dx, 4), lax.rem(my_y + dy, 4)
+
+    plane = [shifted(d // 4, d % 4) for d in range(1, 16)]
+    origin = [shifted(4 - d // 4, 4 - d % 4) for d in range(1, 16)]
+    plane_row = [(x * 2 + my_c, my_z * 4 + y) for x, y in plane]
     row_z = [(strip, lax.rem(my_z + d, 8) * 4 + my_y) for d in range(1, 8)]
-    peers = near + [mate] + row_x + row_y + row_z
+    peers = near + [mate] + plane_row + row_z
 
     pairs = [
         (nodes_hbm, nodes_ref),
@@ -188,6 +192,8 @@
     agg_ref[...] = jnp.zeros_like(agg_ref)
     gsum_ref[...] = jnp.zeros_like(gsum_ref)
     part_ref[2 * H : 4 * H, :] = jnp.zeros((2 * H, H), F32)
+    for k in (3, 7, 11, 15):
+        p_out[k, 16:32, :] = jnp.zeros((16, H), BF16)
 
     pl.semaphore_wait(barrier, len(peers))
     halo_copies = [
@@ -342,9 +348,7 @@
     for copy in returned:
         copy.start()
     node_grad_ref[...] += dot_nt(g_s, w_s) + dot_nt(g_r, w_r)
-    mine = part_ref[pl.ds(my_c * half, half), :]
     core.wait()
-    acc = mine + c_land[...].astype(F32)
 
     def share(src, dst, base, row):
         copies = [
@@ -355,28 +359,23 @@
             copy.start()
         return copies
 
-    piece = half // 4
-    x_out[...] = acc.reshape(4, piece, H).astype(BF16)
-    copies = share(lambda d: x_out.at[lax.rem(my_x + d, 4)], lambda d: x_land.at[d - 1], 0, row_x)
-    for copy in copies:
-        copy.wait()
-    acc = x_out[my_x].astype(F32)
-    for d in range(3):
-        acc = acc + x_land[d].astype(F32)
-
-    for k in range(4):
-        low, high = 32 * k, min(32 * k + 32, piece)
-        y_out[k, 0 : high - low, :] = acc[low:high, :].astype(BF16)
-    y_out[3, 16:32, :] = jnp.zeros((16, H), BF16)
-    copies = share(lambda d: y_out.at[lax.rem(my_y + d, 4)], lambda d: y_land.at[d - 1], 3, row_y)
-    for copy in copies:
-        copy.wait()
-    acc = y_out[my_y].astype(F32)
-    for d in range(3):
-        acc = acc + y_land[d].astype(F32)
+    for k, (low, size) in enumerate(PIECES):
+        mine = part_ref[pl.ds(my_c * half + low, size), :]
+        p_out[k, 0:size, :] = (mine + c_land[low : low + size, :].astype(F32)).astype(BF16)
+    my_p = my_x * 4 + my_y
+    copies = share(
+        lambda d: p_out.at[plane[d - 1][0] * 4 + plane[d - 1][1]],
+        lambda d: p_land.at[d - 1],
+        0,
+        plane_row,
+    )
+    acc = p_out[my_p].astype(F32)
+    for d in FROM_NEAR:
+        copies[d - 1].wait()
+        acc = acc + p_land[d - 1].astype(F32)
 
     z_out[...] = acc.astype(BF16)
-    copies = share(lambda d: z_out, lambda d: z_land.at[my_z], 6, row_z)
+    copies = share(lambda d: z_out, lambda d: z_land.at[my_z], 15, row_z)
     z_land[my_z] = z_out[...]
 
     for copy in returned:
@@ -394,19 +393,23 @@
     for k in range(1, 8):
         acc = acc + z_land[k].astype(F32)
 
-    y_all[my_y] = acc.astype(BF16)
-    copies = share(lambda d: y_all.at[my_y], lambda d: y_all.at[my_y], 13, row_y)
-    for copy in copies:
+    def pass_on(k, p):
+        piece = all_ref.at[my_c, p]
+        copy = remote(piece, piece, send_sem.at[38 + k], recv_sem.at[38 + k], mate)
+        copy.start()
+        return copy
+
+    all_ref[my_c, my_p] = acc.astype(BF16)
+    copies = share(
+        lambda d: all_ref.at[my_c, my_p], lambda d: all_ref.at[my_c, my_p], 22, plane_row
+    )
+    passed = [pass_on(0, my_p)]
+    for d in FROM_NEAR:
+        copies[d - 1].wait()
+        passed.append(pass_on(d, origin[d - 1][0] * 4 + origin[d - 1][1]))
+    for copy in passed:
         copy.wait()
-    x_all[my_x] = y_all[...].reshape(128, H)[0:piece, :]
-    copies = share(lambda d: x_all.at[my_x], lambda d: x_all.at[my_x], 16, row_x)
-    for copy in copies:
-        copy.wait()
-    c_all[my_c] = x_all[...].reshape(half, H)
-    core = remote(c_all.at[my_c], c_all.at[my_c], send_sem.at[20], recv_sem.at[20], mate)
-    core.start()
-    core.wait()
-    stores.append(pltpu.make_async_copy(c_all, total_hbm, store_sem.at[3]))
+    stores.append(pltpu.make_async_copy(all_ref, total_hbm, store_sem.at[3]))
     stores[3].start()
     for store in stores:
         store.wait()
@@ -436,7 +439,7 @@
             jax.ShapeDtypeStruct((n_p, H), BF16),
             jax.ShapeDtypeStruct((n_e, H), BF16),
             jax.ShapeDtypeStruct((n_p, H), F32),
-            jax.ShapeDtypeStruct((2, half, H), BF16),
+            jax.ShapeDtypeStruct((2, 16, 32, H), BF16),
         ),
         in_specs=[hbm()] * 11,
         out_specs=[hbm()] * 4,
@@ -469,17 +472,13 @@
             pltpu.VMEM((7 * H, H), F32),
             pltpu.VMEM((half, H), BF16),
             pltpu.VMEM((half, H), BF16),
-            pltpu.VMEM((4, half // 4, H), BF16),
-            pltpu.VMEM((3, half // 4, H), BF16),
-            pltpu.VMEM((4, 32, H), BF16),
-            pltpu.VMEM((3, 32, H), BF16),
+            pltpu.VMEM((16, 32, H), BF16),
+            pltpu.VMEM((15, 32, H), BF16),
             pltpu.VMEM((32, H), BF16),
             pltpu.VMEM((8, 32, H), BF16),
-            pltpu.VMEM((4, 32, H), BF16),
-            pltpu.VMEM((4, half // 4, H), BF16),
-            pltpu.VMEM((2, half, H), BF16),
-            dma((21,)),
-            dma((21,)),
+            pltpu.VMEM((2, 16, 32, H), BF16),
+            dma((54,)),
+            dma((54,)),
         ],
         compiler_params=pltpu.CompilerParams(
             collective_id=0, has_side_effects=True, vmem_limit_bytes=62_000_000
@@ -526,9 +525,11 @@
         taken[-1].start()
 
     brought[0].wait()
-    half = total_buf.shape[1]
-    grad_buf[0:half, :] = total_buf[0].astype(F32) * factor
-    grad_buf[half:, :] = total_buf[1].astype(F32) * factor
+    half = grad_buf.shape[0] // 2
+    for c in range(2):
+        for k, (low, size) in enumerate(PIECES):
+            rows = pl.ds(c * half + low, size)
+            grad_buf[rows, :] = total_buf[c, k, 0:size, :].astype(F32) * factor
     first = 0
     for out in (ei_out, eo_out, ni_out, no_out):
         take(grad_buf.at[pl.ds(first, out.shape[0]), :], out)

time: 51 us -> 47.3 us (0.927)
  Pallas kernels: 49.6 us -> 45.8 us
    pallas_call x1, Pallas kernels: 47.3 us -> 43.5 us  [step_call(): pl.pallas_call(functools.partial(step_kernel, sizes), out_shape=(jax.Shap...]
where the time goes in v3:
time: 47.3 us; the launch traced here: 47.1 us
  Pallas kernels  45.8 us (97%)
  between operations  1.29 us (3%)
    pallas_call x1, Pallas kernels, step_call(): pl.pallas_call(functools.partial(step_kernel, sizes), out_shape=(jax.Shap...  43.5 us
    pallas_call x1, Pallas kernels, finish_call(): pl.pallas_call(functools.partial(finish_kernel, factor), out_shape=tuple(...  2.3 us

profile of v3, /device:TPU:1, one launch (start us, length us, event | category | flops | bytes accessed | tf_op | source)
XLA Modules:
  0.0 47.1 jit_solution(2338216264027910961)
XLA Ops:
  1.3 43.5 %shard_map.162 = (bf16[256,128]{1,0:T(8,128)(2,1)}, bf16[4096,128]{1,0:T(8,128)(2,1)}, f32[256,128]{1,0:T(8,128)}, bf16[2,16,32,128]{3,2,1,0:T(8,128)(2,1)}) custom-call(bf16[256,128]{1,0:T(8,128)(2,1)} %nodes_hbm.1, bf16[4096,128]{1,0:T(8,128)(2,1)} %edges_hbm.1, s32[32,128]{1,0:T(8,128)} %bitcast.2, s32[32,128]{1,0:T(8,128)} %bitcast.3, ...), custom_call_target="tpu_custom_call" | custom-call | tf_op jit(solution)/shard_map/pallas_call | solution.py:436
  44.8 2.3 %shard_map.163 = (bf16[256,128]{1,0:T(8,128)(2,1)}, bf16[4096,128]{1,0:T(8,128)(2,1)}, f32[256,128]{1,0:T(8,128)}, f32[384,128]{1,0:T(8,128)}, f32[128,128]{1,0:...) custom-call(bf16[256,128]{1,0:T(8,128)(2,1)} %get-tuple-element.11.nn_ref, bf16[4096,128]{1,0:T(8,128)(2,1)} %get-tuple-element.12.ne_ref, ...), custom_call_target="tpu_custom_call" | custom-call | tf_op jit(solution)/shard_map/pallas_call | solution.py:558

commit v4 on v3

--- a/solution.py
+++ b/solution.py
@@ -19,6 +19,7 @@
 PIECES = [(112 * (k // 4) + 32 * (k % 4), 16 if k % 4 == 3 else 32) for k in range(16)]
 HOPS = [min(d // 4, 4 - d // 4) + min(d % 4, 4 - d % 4) for d in range(16)]
 FROM_NEAR = sorted(range(1, 16), key=lambda d: HOPS[d])
+SHIFTS = (2, 1, 3, 0)
 NEAR = [(ds, dj) for ds in (-1, 0, 1) for dj in (-1, 0, 1) if (ds, dj) != (0, 0)]
 
 
@@ -337,19 +338,25 @@
     part_ref[H : 2 * H, :] = dot_tn(nodes, g_r)
 
     half = c_out.shape[0]
-    c_out[...] = part_ref[pl.ds((1 - my_c) * half, half), :].astype(BF16)
-    core = remote(c_out, c_land, send_sem.at[0], recv_sem.at[0], mate)
-    core.start()
+    part = half // 4
+
+    def chip_rows(dx, base):
+        return pl.ds(pl.multiple_of(base * half + lax.rem(my_x + dx, 4) * part, 16), part)
+
+    core = {}
+    for k, dx in enumerate(SHIFTS):
+        rows = chip_rows(dx, 0)
+        c_out[rows, :] = part_ref[chip_rows(dx, 1 - my_c), :].astype(BF16)
+        core[dx] = remote(
+            c_out.at[rows, :], c_land.at[rows, :], send_sem.at[54 + k], recv_sem.at[54 + k], mate
+        )
+        core[dx].start()
     owed_ref[...] = dot_nt(g_h, w_s).astype(BF16).reshape(8, border, H)
     returned = [
         remote(owed_ref.at[k], back_ref.at[7 - k], near_sem.at[2, k], near_sem.at[3, 7 - k], peer)
         for k, peer in enumerate(near)
     ]
-    for copy in returned:
-        copy.start()
     node_grad_ref[...] += dot_nt(g_s, w_s) + dot_nt(g_r, w_r)
-    core.wait()
-
     def share(src, dst, base, row):
         copies = [
             remote(src(d), dst(d), send_sem.at[base + d], recv_sem.at[base + d], peer)
@@ -359,19 +366,27 @@
             copy.start()
         return copies
 
-    for k, (low, size) in enumerate(PIECES):
-        mine = part_ref[pl.ds(my_c * half + low, size), :]
-        p_out[k, 0:size, :] = (mine + c_land[low : low + size, :].astype(F32)).astype(BF16)
     my_p = my_x * 4 + my_y
-    copies = share(
-        lambda d: p_out.at[plane[d - 1][0] * 4 + plane[d - 1][1]],
-        lambda d: p_land.at[d - 1],
-        0,
-        plane_row,
-    )
+    copies = {}
+    for dx in SHIFTS:
+        core[dx].wait()
+        total = part_ref[chip_rows(dx, my_c), :] + c_land[chip_rows(dx, 0), :].astype(F32)
+        for k, (low, size) in enumerate(PIECES[0:4]):
+            p_out[lax.rem(my_x + dx, 4) * 4 + k, 0:size, :] = total[low : low + size, :].astype(BF16)
+        for d in range(max(dx * 4, 1), dx * 4 + 4):
+            copies[d] = remote(
+                p_out.at[plane[d - 1][0] * 4 + plane[d - 1][1]],
+                p_land.at[d - 1],
+                send_sem.at[d],
+                recv_sem.at[d],
+                plane_row[d - 1],
+            )
+            copies[d].start()
+    for copy in returned:
+        copy.start()
     acc = p_out[my_p].astype(F32)
     for d in FROM_NEAR:
-        copies[d - 1].wait()
+        copies[d].wait()
         acc = acc + p_land[d - 1].astype(F32)
 
     z_out[...] = acc.astype(BF16)
@@ -477,8 +492,8 @@
             pltpu.VMEM((32, H), BF16),
             pltpu.VMEM((8, 32, H), BF16),
             pltpu.VMEM((2, 16, 32, H), BF16),
-            dma((54,)),
-            dma((54,)),
+            dma((58,)),
+            dma((58,)),
         ],
         compiler_params=pltpu.CompilerParams(
             collective_id=0, has_side_effects=True, vmem_limit_bytes=62_000_000

time: 47.3 us -> 47.2 us (level)
  no operation moved by 1% of the time
where the time goes in v4:
time: 47.2 us; the launch traced here: 47 us
  Pallas kernels  45.7 us (97%)
  between operations  1.29 us (3%)
    pallas_call x1, Pallas kernels, step_call(): pl.pallas_call(functools.partial(step_kernel, sizes), out_shape=(jax.Shap...  43.4 us
    pallas_call x1, Pallas kernels, finish_call(): pl.pallas_call(functools.partial(finish_kernel, factor), out_shape=tuple(...  2.3 us

profile of v4, /device:TPU:1, one launch (start us, length us, event | category | flops | bytes accessed | tf_op | source)
XLA Modules:
  0.0 47.0 jit_solution(12008326879323483159)
XLA Ops:
  1.3 43.4 %shard_map.162 = (bf16[256,128]{1,0:T(8,128)(2,1)}, bf16[4096,128]{1,0:T(8,128)(2,1)}, f32[256,128]{1,0:T(8,128)}, bf16[2,16,32,128]{3,2,1,0:T(8,128)(2,1)}) custom-call(bf16[256,128]{1,0:T(8,128)(2,1)} %nodes_hbm.1, bf16[4096,128]{1,0:T(8,128)(2,1)} %edges_hbm.1, s32[32,128]{1,0:T(8,128)} %bitcast.2, s32[32,128]{1,0:T(8,128)} %bitcast.3, ...), custom_call_target="tpu_custom_call" | custom-call | tf_op jit(solution)/shard_map/pallas_call | solution.py:451
  44.7 2.3 %shard_map.163 = (bf16[256,128]{1,0:T(8,128)(2,1)}, bf16[4096,128]{1,0:T(8,128)(2,1)}, f32[256,128]{1,0:T(8,128)}, f32[384,128]{1,0:T(8,128)}, f32[128,128]{1,0:...) custom-call(bf16[256,128]{1,0:T(8,128)(2,1)} %get-tuple-element.11.nn_ref, bf16[4096,128]{1,0:T(8,128)(2,1)} %get-tuple-element.12.ne_ref, ...), custom_call_target="tpu_custom_call" | custom-call | tf_op jit(solution)/shard_map/pallas_call | solution.py:573
